TPU v7x, 32 devices: a whole 2x2x4 slice. The times are simulated.
32 devices in a mesh: req: 8 (over z, y), tp: 4 (over x, core).
Axes of the slice: x: 2, y: 2, z: 4, core: 2. Of those that a mesh axis runs over, the one named last changes fastest.
Arguments:
- hidden: bfloat16 [2048, 5120], P('req', 'tp'), may hold values from -200 to 200
- norm_gain: bfloat16 [5120], replicated, may hold values from 0.099609375 to 1.8984375
- wq: bfloat16 [5120, 4096], P(None, 'tp'), may hold values from -0.078125 to 0.078125
- wkv: bfloat16 [5120, 2, 1024], P(None, None, 'tp'), may hold values from -0.15625 to 0.15625
- wo: bfloat16 [4096, 5120], P('tp'), may hold values from -1 to 1
- perm: int32 [16], replicated, may hold values from 0 to 15, as said below
- prior_len: int32 [16], P('req'), may hold values from 128 to 8192, as said below
- page_table: int32 [16, 64], P('req'), may hold values from 0 to 127, as said below
- pool: bfloat16 [1024, 128, 2, 1024], P('req', None, None, 'tp'), may hold values from -400 to 400
- send_table: int32 [8, 8, 17], P('req'), may hold values from -1 to 129, as said below
Outputs:
- attn_out: bfloat16 [2048, 5120], P('req', 'tp')
- decode_cache: bfloat16 [8, 8, 17, 128, 2, 1024], P('req', None, None, None, None, 'tp')
Inputs may be any that keep to these rules, and one draw needn't show every extreme that they name: `perm`: a permutation of the requests. `prior_len`: one request has exactly 8192 cached tokens and another exactly 128. `page_table`: row r names pages of the pool block of the device that holds the dealt slot of request r; the rows of the 2 requests dealt to one device name all different pages. `send_table`: codes l * 65 + p name updated page p of slot l of the sending device, -1 an empty slot; every page p < (lengths + 255) // 128 of each of its slots is named exactly once in the sending device's row, no other page is named, and in every draw some block is full.
All inputs are finite; a program needn't handle non-finite values.
Results may differ from a plain program's by a relative error of at most 0.013.
The roundings to bfloat16 on the way count: a program that leaves them out, or rounds other values in their place, can miss the bound.
Values may be sent and summed in bfloat16 or wider, within the bound.
A program may use at most 256 MiB of HBM per device.

v0:
```python
import math

import jax
import jax.numpy as jnp
from jax import lax
from jax.experimental import pallas as pl
from jax.experimental.pallas import tpu as pltpu
from jax.sharding import PartitionSpec as P

HEAD_SIZE = 128
NORM_EPSILON = 1e-05
ROPE_THETA = 100000000.0
BLOCK_PAGES = 4


def normalize(rows, gain):
    wide_rows = rows.astype(jnp.float32)
    mean_square = jnp.mean(wide_rows * wide_rows, axis=-1, keepdims=True)
    return (wide_rows * lax.rsqrt(mean_square + NORM_EPSILON) * gain.astype(jnp.float32)).astype(
        jnp.bfloat16
    )


def rotate(vectors, positions):
    half_size = vectors.shape[-1] // 2
    frequency = jnp.power(
        jnp.float32(ROPE_THETA), -2.0 * jnp.arange(half_size, dtype=jnp.float32) / vectors.shape[-1]
    )
    angles = positions.astype(jnp.float32)[:, None] * frequency[None, :]
    cosine = jnp.cos(angles)[:, None, :]
    sine_part = jnp.sin(angles)[:, None, :]
    first_half = vectors[..., :half_size]
    second_half = vectors[..., half_size:]
    return jnp.concatenate(
        [
            first_half * cosine - second_half * sine_part,
            second_half * cosine + first_half * sine_part,
        ],
        axis=-1,
    )


class Layout:
    def __init__(self, slots, row_pages, peers, block):
        self.slots, self.row_pages, self.peers, self.block = slots, row_pages, peers, block
        self.code_width = row_pages + 1
        self.sends = slots + slots * row_pages
        self.width = self.sends + peers * block

    def request(self, perm, device, slot):
        request = perm[device * self.slots + slot]
        return (request // self.slots) * self.width, request % self.slots

    def length(self, table, perm, device, slot):
        base, row = self.request(perm, device, slot)
        return table[base + row]

    def physical(self, table, perm, device, slot, page):
        base, row = self.request(perm, device, slot)
        return table[base + self.slots + row * self.row_pages + jnp.minimum(page, self.row_pages - 1)]

    def code(self, table, source, target, number):
        return table[source * self.width + self.sends + target * self.block + number]


def pack_kernel(layout, table, perm, me, pool, out, sem):
    def send(index, carry):
        target, number = index // layout.block, index % layout.block
        code = jnp.maximum(layout.code(table, me[0], target, number), 0)
        page = layout.physical(
            table, perm, me[0], code // layout.code_width, code % layout.code_width
        )
        pltpu.make_async_copy(pool.at[page], out.at[target, number], sem).start()
        return carry

    lax.fori_loop(0, layout.peers * layout.block, send, 0)
    pltpu.make_async_copy(out, out, sem).wait()


def pack_pages(layout, table, perm, me, pool):
    return pl.pallas_call(
        lambda *refs: pack_kernel(layout, *refs),
        out_shape=jax.ShapeDtypeStruct((layout.peers, layout.block) + pool.shape[1:], pool.dtype),
        grid_spec=pltpu.PrefetchScalarGridSpec(
            num_scalar_prefetch=3,
            grid=(1,),
            in_specs=[pl.BlockSpec(memory_space=pl.ANY)],
            out_specs=pl.BlockSpec(memory_space=pl.ANY),
            scratch_shapes=[pltpu.SemaphoreType.DMA],
        ),
        name="pack_pages",
    )(table, perm, me, pool)


def finish_kernel(layout, table, perm, me, arrived, recent, zeros, out, sem):
    page_len = out.shape[2]

    def rows(source, source_row, target, target_row, count):
        size = page_len
        while size:
            offset = count // (2 * size) * (2 * size)

            @pl.when(count // size % 2 == 1)
            def _(size=size, offset=offset):
                pltpu.make_async_copy(
                    source.at[pl.ds(source_row + offset, size)],
                    target.at[pl.ds(target_row + offset, size)],
                    sem,
                ).start()

            size //= 2

    def place(index, carry):
        source, number = index // layout.block, index % layout.block
        raw_code = layout.code(table, source, me[0], number)
        code = jnp.maximum(raw_code, 0)
        slot, page = code // layout.code_width, code % layout.code_width
        length = layout.length(table, perm, source, slot)
        full, kept = length // page_len, length % page_len
        target = out.at[source, number]
        valid = raw_code >= 0

        @pl.when(valid & (page < full))
        def _():
            pltpu.make_async_copy(arrived.at[source, number], target, sem).start()

        @pl.when(jnp.logical_not(valid) | (page > full + 1))
        def _():
            pltpu.make_async_copy(zeros, target, sem).start()

        @pl.when(valid & (page == full))
        def _():
            rows(arrived.at[source, number], 0, target, 0, kept)
            rows(recent.at[source, slot], 0, target, kept, page_len - kept)

        @pl.when(valid & (page == full + 1))
        def _():
            rows(recent.at[source, slot], page_len - kept, target, 0, kept)
            rows(zeros, 0, target, kept, page_len - kept)

        return carry

    lax.fori_loop(0, layout.peers * layout.block, place, 0)
    pltpu.make_async_copy(out, out, sem).wait()


def finish_pages(layout, table, perm, me, arrived, recent):
    zeros = jnp.zeros(arrived.shape[2:], arrived.dtype)
    return pl.pallas_call(
        lambda *refs: finish_kernel(layout, *refs),
        out_shape=jax.ShapeDtypeStruct(arrived.shape, arrived.dtype),
        grid_spec=pltpu.PrefetchScalarGridSpec(
            num_scalar_prefetch=3,
            grid=(1,),
            in_specs=[pl.BlockSpec(memory_space=pl.ANY)] * 3,
            out_specs=pl.BlockSpec(memory_space=pl.ANY),
            scratch_shapes=[pltpu.SemaphoreType.DMA],
        ),
        name="finish_pages",
    )(table, perm, me, arrived, recent, zeros)


def attend_kernel(lengths, tables, q_ref, nk_ref, nv_ref, *rest):
    k_refs, v_refs = rest[:BLOCK_PAGES], rest[BLOCK_PAGES : 2 * BLOCK_PAGES]
    out_ref, q_rows, top, total, acc = rest[2 * BLOCK_PAGES :]
    kv_heads, rows, head = q_rows.shape
    tokens = q_ref.shape[0]
    groups = rows // tokens
    slot, step = pl.program_id(0), pl.program_id(1)
    page_len = k_refs[0].shape[1]
    block_keys = BLOCK_PAGES * page_len
    length = lengths[slot]
    inv_scale = 1.0 / math.sqrt(head)

    def score(kv, keys):
        return (
            lax.dot_general(
                q_rows[kv], keys, (((1,), (1,)), ((), ())), preferred_element_type=jnp.float32
            )
            * inv_scale
        )

    @pl.when(step == 0)
    def _():
        for kv in range(kv_heads):
            columns = slice(kv * head, (kv + 1) * head)
            for group in range(groups):
                lane = (kv * groups + group) * head
                q_rows[kv, group * tokens : (group + 1) * tokens, :] = q_ref[:, lane : lane + head]
            scores = score(kv, nk_ref[:, columns])
            query_id = lax.broadcasted_iota(jnp.int32, scores.shape, 0) % tokens
            key_id = lax.broadcasted_iota(jnp.int32, scores.shape, 1)
            scores = jnp.where(key_id <= query_id, scores, -1e30)
            highest = jnp.max(scores, axis=-1, keepdims=True)
            weights = jnp.exp(scores - highest)
            top[kv] = jnp.broadcast_to(highest, (rows, head))
            total[kv] = jnp.broadcast_to(jnp.sum(weights, axis=-1, keepdims=True), (rows, head))
            acc[kv] = jnp.dot(
                weights.astype(jnp.bfloat16), nv_ref[:, columns], preferred_element_type=jnp.float32
            )

    @pl.when(step * block_keys < length)
    def _():
        for kv in range(kv_heads):
            columns = slice(kv * head, (kv + 1) * head)
            keys = jnp.concatenate([ref[0, :, columns] for ref in k_refs], axis=0)
            values = jnp.concatenate([ref[0, :, columns] for ref in v_refs], axis=0)
            scores = score(kv, keys)
            key_id = lax.broadcasted_iota(jnp.int32, scores.shape, 1)
            scores = jnp.where(key_id < length - step * block_keys, scores, -1e30)
            before = top[kv]
            highest = jnp.maximum(before, jnp.max(scores, axis=-1, keepdims=True))
            factor = jnp.exp(before - highest)
            weights = jnp.exp(scores - highest[:, :1])
            top[kv] = highest
            total[kv] = total[kv] * factor + jnp.sum(weights, axis=-1, keepdims=True)
            acc[kv] = acc[kv] * factor + jnp.dot(
                weights.astype(jnp.bfloat16), values, preferred_element_type=jnp.float32
            )

    @pl.when(step == pl.num_programs(1) - 1)
    def _():
        for kv in range(kv_heads):
            context = (acc[kv] / total[kv]).astype(jnp.bfloat16)
            for group in range(groups):
                lane = (kv * groups + group) * head
                out_ref[:, lane : lane + head] = context[group * tokens : (group + 1) * tokens]


def attend(lengths, tables, queries, new_keys, new_values, k_pool, v_pool):
    slots, row_pages = tables.shape
    tokens = queries.shape[0] // slots
    page_len, features = k_pool.shape[1:]
    kv_heads = features // HEAD_SIZE
    rows = tokens * (queries.shape[1] // features)
    steps = row_pages // BLOCK_PAGES

    def page_spec(number):
        def pick(slot, step, lengths, tables):
            last = (lengths[slot] + page_len - 1) // page_len - 1
            return (tables[slot * row_pages + jnp.minimum(step * BLOCK_PAGES + number, last)], 0, 0)

        return pl.BlockSpec((1, page_len, features), pick)

    def slot_rows(slot, step, lengths, tables):
        return (slot, 0)

    pages = [page_spec(number) for number in range(BLOCK_PAGES)]
    state = pltpu.VMEM((kv_heads, rows, HEAD_SIZE), jnp.float32)
    return pl.pallas_call(
        attend_kernel,
        out_shape=jax.ShapeDtypeStruct(queries.shape, jnp.bfloat16),
        grid_spec=pltpu.PrefetchScalarGridSpec(
            num_scalar_prefetch=2,
            grid=(slots, steps),
            in_specs=[
                pl.BlockSpec((tokens, queries.shape[1]), slot_rows),
                pl.BlockSpec((tokens, features), slot_rows),
                pl.BlockSpec((tokens, features), slot_rows),
            ]
            + pages
            + pages,
            out_specs=pl.BlockSpec((tokens, queries.shape[1]), slot_rows),
            scratch_shapes=[
                pltpu.VMEM((kv_heads, rows, HEAD_SIZE), jnp.bfloat16),
                state,
                state,
                state,
            ],
        ),
        compiler_params=pltpu.CompilerParams(
            dimension_semantics=("arbitrary", "arbitrary"), vmem_limit_bytes=40 << 20
        ),
        name="attend",
    )(
        lengths,
        tables.reshape(-1),
        queries,
        new_keys,
        new_values,
        *([k_pool] * BLOCK_PAGES),
        *([v_pool] * BLOCK_PAGES),
    )


def shards(hidden, norm_gain, wq, wkv, wo, perm, prior_len, page_table, pool, send_table):
    slots = prior_len.shape[0]
    tokens = hidden.shape[0] // slots
    _, peers, block = send_table.shape
    layout = Layout(slots, page_table.shape[1], peers, block)
    features = pool.shape[-1]
    device = lax.axis_index("req")
    me = device.astype(jnp.int32).reshape(1)
    mine = jnp.concatenate([prior_len, page_table.reshape(-1), send_table.reshape(-1)])
    table = lax.all_gather(mine, "req", axis=0, tiled=True)
    outgoing = pack_pages(layout, table, perm, me, pool)
    arrived = lax.all_to_all(outgoing, "req", split_axis=0, concat_axis=0, tiled=True)

    full_rows = lax.all_gather(hidden, "tp", axis=1, tiled=True)
    late_pool, wkv, outgoing = lax.optimization_barrier((pool, wkv, outgoing))
    requests = lax.dynamic_slice_in_dim(perm, device * slots, slots)
    by_device = table.reshape(peers, layout.width)
    lengths = by_device[:, :slots].reshape(-1)[requests]
    tables = by_device[:, slots : layout.sends].reshape(-1, layout.row_pages)[requests]

    normalized_input = normalize(full_rows, norm_gain)
    query_proj = jnp.dot(normalized_input, wq, preferred_element_type=jnp.float32)
    pair_proj = jnp.dot(
        normalized_input, wkv.reshape(wkv.shape[0], -1), preferred_element_type=jnp.float32
    )
    positions = (lengths[:, None] + jnp.arange(tokens, dtype=jnp.int32)[None, :]).reshape(-1)
    queries = rotate(query_proj.reshape(query_proj.shape[0], -1, HEAD_SIZE), positions).astype(
        jnp.bfloat16
    )
    pair_heads = pair_proj.reshape(pair_proj.shape[0], 2, -1, HEAD_SIZE)
    new_keys = rotate(pair_heads[:, 0], positions).astype(jnp.bfloat16).reshape(-1, features)
    new_values = pair_heads[:, 1].astype(jnp.bfloat16).reshape(-1, features)
    recent = jnp.stack([new_keys, new_values], axis=1).reshape(slots, tokens, 2, features)
    all_recent = lax.all_gather(recent, "req", axis=0)

    context = attend(
        lengths,
        tables,
        queries.reshape(queries.shape[0], -1),
        new_keys,
        new_values,
        late_pool[:, :, 0],
        late_pool[:, :, 1],
    )
    partial_value = jnp.dot(context, wo, preferred_element_type=jnp.float32)
    attn_out = lax.psum_scatter(
        partial_value.astype(jnp.bfloat16), "tp", scatter_dimension=1, tiled=True
    )
    decode_pages = finish_pages(layout, table, perm, me, arrived, all_recent)
    return (attn_out, decode_pages[None])


def solution(mesh):
    placed = (
        P("req", "tp"),
        P(),
        P(None, "tp"),
        P(None, None, "tp"),
        P("tp", None),
        P(),
        P("req"),
        P("req", None),
        P("req", None, None, "tp"),
        P("req", None, None),
    )
    return jax.shard_map(
        shards,
        mesh=mesh,
        in_specs=placed,
        out_specs=(P("req", "tp"), P("req", None, None, None, None, "tp")),
        check_vma=False,
    )
```

profile of v0, /device:TPU:0, one launch (start us, length us, event | category | flops | bytes accessed | tf_op | source)
XLA Modules:
  0.0 1551.2 jit_solution(7103475778477914452)
XLA Ops:
  7.2 0.8 reshape.145
  7.9 0.8 reshape.146
  8.7 1.2 dynamic-slice
  10.6 0.8 add_dynamic-update-slice_fusion
  11.4 38.8 %all-reduce.refs_0_ = s32[2128]{0:T(1024)} all-reduce(s32[2128]{0:T(1024)S(1)} %add_dynamic-update-slice_fusion), channel_id=1, replica_groups=mesh['req'=8,'tp'=4] {'req'}, use_global_device_ids=true, to_apply=%add | all-reduce | flops 2128 | bytes 17024
  50.3 541.9 %pack_pages.1 = bf16[8,17,128,2,256]{4,3,2,1,0:T(2,128)(2,1)} custom-call(s32[2128]{0:T(1024)} %all-reduce.refs_0_, s32[16]{0:T(128)} %refs_1_.3, s32[1]{0:T(128)} %bitcast.4.refs_2_, bf16[128,128,2,256]{3,2,1,0:T(2,128)(2,1)} %refs_3_.1), custom_call_target="tpu_custom_call" | custom-call | tf_op jit(solution)/shard_map/pack_pages/pallas_call | solution.py:81
  592.3 6.0 all-to-all-start
  598.3 0.7 all-gather.3.cloned.1.call-update
  599.4 0.6 gather_fusion
  600.1 0.6 gather_fusion.1
  600.8 0.3 multiply_cosine_fusion
  601.3 5.7 copy.50
  607.1 7.7 copy.34
  614.8 15.4 copy.37
  630.2 2.3 fusion
  632.5 4.9 fusion.3
  637.6 0.1 copy.46
  637.9 0.7 copy.41
  638.6 0.2 reduce-scatter.2.cloned.1.call-start
  638.9 12.0 slice_bitcast_fusion
  650.9 5.7 convolution_bitcast_fusion
  656.5 0.2 copy.48
  656.8 0.5 subtract_convert_fusion
  657.2 0.3 pad_maximum_fusion
  657.9 3.4 copy-done
  661.3 49.7 %attend.1 = bf16[256,1024]{1,0:T(8,128)(2,1)S(1)} custom-call(s32[2]{0:T(128)S(1)} %gather_fusion, s32[128]{0:T(128)S(1)} %reshape.150.tables, bf16[256,1024]{1,0:T(8,128)(2,1)S(1)} %bitcast.40, bf16[256,256]{1,0:T(8,128)(2,1)S(1)} %copy.44.nk_ref, bf16[256,256]{1,0:T(8,128)(2,1)S(1)} %copy.45.nv_ref, bf16[128,128,256]{2,1,0:T(8,128)(2,1)S(1)} %copy-done, ...), custom_call_target="tpu_custom_call" | custom-call | tf_op jit(solution)/shard_map/attend/pallas_call | solution.py:250
  711.0 8.2 convolution_convert_fusion
  719.2 197.3 %all-gather.5.cloned.1.call-done = bf16[8,2,128,2,256]{4,2,3,1,0:T(8,128)(2,1)} async-done(((bf16[1,2,128,2,256]{4,2,3,1,0:T(8,128)(2,1)}), bf16[8,2,128,2,256]{4,2,3,1,0:T(8,128)(2,1)}) %all-gather.5.cloned.1.call-update) | async-done | bytes 2097168 | tf_op jit(solution)/shard_map/all_gather | solution.py:319
  916.5 5.1 copy.42.refs_4_
  921.6 80.4 %all-to-all-done.refs_3_ = bf16[8,17,128,2,256]{4,3,2,1,0:T(2,128)(2,1)} async-done(((bf16[8,17,128,2,256]{4,3,2,1,0:T(2,128)(2,1)}), bf16[8,17,128,2,256]{4,3,2,1,0:T(2,128)(2,1)}, u32[]{:S(2)}, u32[]{:S(2)}) %all-to-all-start) | async-done | bytes 17825824 | tf_op jit(solution)/shard_map/all_to_all | solution.py:297
  1002.0 0.7 broadcast_in_dim.7.refs_5_
  1002.7 542.0 %finish_pages.1 = bf16[8,17,128,2,256]{4,3,2,1,0:T(2,128)(2,1)} custom-call(s32[2128]{0:T(1024)} %all-reduce.refs_0_, s32[16]{0:T(128)} %refs_1_.3, s32[1]{0:T(128)} %bitcast.4.refs_2_, bf16[8,17,128,2,256]{4,3,2,1,0:T(2,128)(2,1)} %all-to-all-done.refs_3_, bf16[8,2,128,2,256]{4,3,2,1,0:T(2,128)(2,1)} %copy.42.refs_4_, ...), custom_call_target="tpu_custom_call" | custom-call | tf_op jit(solution)/shard_map/finish_pages/pallas_call | solution.py:149
  (41 shorter events, 1.5 us)
Async XLA Ops:
  592.2 6.8 copy-start.2
  592.2 7.1 copy-start.4
  592.3 8.5 copy-start.3
  592.3 409.7 %all-to-all-start = ((bf16[8,17,128,2,256]{4,3,2,1,0:T(2,128)(2,1)}), bf16[8,17,128,2,256]{4,3,2,1,0:T(2,128)(2,1)}, u32[]{:S(2)}, u32[]{:S(2)}) async-start(bf16[8,17,128,2,256]{4,3,2,1,0:T(2,128)(2,1)} %pack_pages.1), calls=%async_computation.1 | async-start | bytes 35651584 | tf_op jit(solution)/shard_map/all_to_all | solution.py:297
  598.3 31.9 %all-gather.3.cloned.1.call-start = ((), (), s32[]{:S(2)}) async-start(), calls=%async_computation.2 | async-start | bytes 3276800 | tf_op jit(solution)/shard_map/all_gather | solution.py:299
  599.0 317.5 %all-gather.5.cloned.1.call-start = ((), (), s32[]{:S(2)}) async-start(), calls=%async_computation.4 | async-start | bytes 2359296 | tf_op jit(solution)/shard_map/all_gather | solution.py:319
  638.6 12.2 copy-start.1
  638.6 906.0 %reduce-scatter.2.cloned.1.call-start = ((), (), s32[]{:S(2)}) async-start(), calls=%async_computation.3 | async-start | bytes 3276800 | tf_op jit(solution)/shard_map/reduce_scatter | solution.py:331
  657.9 3.4 copy-start
Sparse Core Ops, SparseCore 0:
  600.7 26.8 all-gather.2
  638.8 277.6 all-gather.4
  919.6 32.1 reduce-scatter.1
where the time goes:
time: 1550 us
  Pallas kernels  1130 us (73%)
  waiting for transfers between devices  278 us (18%)
  local copies, waits for them, and re-layouts  56.1 us (4%)
  blocking collectives  38.8 us (3%)
  matrix products  18.8 us (1%)
    pallas_call x1, Pallas kernels, finish_pages(): pl.pallas_call(lambda *refs: finish_kernel(layout, *refs), out_shape=jax....  542 us
    pallas_call x1, Pallas kernels, pack_pages(): pl.pallas_call(lambda *refs: pack_kernel(layout, *refs), out_shape=jax.Sh...  542 us
    all_gather x1, waiting for transfers between devices, shards(): all_recent = lax.all_gather(recent, 'req', axis=0)  197 us
    all_to_all x1, waiting for transfers between devices, shards(): lax.all_to_all(outgoing, 'req', split_axis=0, concat_axis=0, tiled=True)  80.4 us
    pallas_call x1, Pallas kernels, attend(): pl.pallas_call(attend_kernel, out_shape=jax.ShapeDtypeStruct(queries.shap...  49.7 us
    unnamed x1, blocking collectives  38.8 us
  transfers between devices with their start and end apart: 4, of which 2 were waited for; matrix products, arithmetic and copies ran while one was open for 5% of the time, Pallas kernels for 38%

commit v1 on v0

--- a/solution.py
+++ b/solution.py
@@ -45,11 +45,14 @@
         self.slots, self.row_pages, self.peers, self.block = slots, row_pages, peers, block
         self.code_width = row_pages + 1
         self.sends = slots + slots * row_pages
-        self.width = self.sends + peers * block
+        self.used = self.sends + peers * block
+        self.width = -(-self.used // 1024) * 1024
+        self.late = 2 * slots
+        self.early = block - self.late
 
     def request(self, perm, device, slot):
         request = perm[device * self.slots + slot]
-        return (request // self.slots) * self.width, request % self.slots
+        return lax.div(request, self.slots) * self.width, lax.rem(request, self.slots)
 
     def length(self, table, perm, device, slot):
         base, row = self.request(perm, device, slot)
@@ -59,105 +62,349 @@
         base, row = self.request(perm, device, slot)
         return table[base + self.slots + row * self.row_pages + jnp.minimum(page, self.row_pages - 1)]
 
-    def code(self, table, source, target, number):
-        return table[source * self.width + self.sends + target * self.block + number]
-
-
-def pack_kernel(layout, table, perm, me, pool, out, sem):
-    def send(index, carry):
-        target, number = index // layout.block, index % layout.block
-        code = jnp.maximum(layout.code(table, me[0], target, number), 0)
-        page = layout.physical(
-            table, perm, me[0], code // layout.code_width, code % layout.code_width
+    def split(self, code):
+        return lax.div(code, self.code_width), lax.rem(code, self.code_width)
+
+    def visit(self, table, perm, source, target, page_len, use):
+        whole = [
+            lax.div(self.length(table, perm, source, slot), page_len) for slot in range(self.slots)
+        ]
+        base = source * self.width + self.sends + target * self.block
+
+        def step(number, counts):
+            plain, tails = counts
+            code = table[base + number]
+            valid = code >= 0
+            slot, page = self.split(jnp.maximum(code, 0))
+            first = whole[0]
+            for other in range(1, self.slots):
+                first = jnp.where(slot == other, whole[other], first)
+            tail = valid & (page >= first)
+            place = jnp.where(valid, jnp.where(tail, self.block - 1 - tails, plain), -1)
+            use(number, code, place)
+            return (
+                plain + jnp.where(valid & jnp.logical_not(tail), 1, 0),
+                tails + jnp.where(tail, 1, 0),
+            )
+
+        lax.fori_loop(0, self.block, step, (jnp.int32(0), jnp.int32(0)))
+
+
+def exchange_kernel(peers, mine, out, send_sems, recv_sems):
+    me = lax.axis_index("req")
+    barrier = pltpu.get_barrier_semaphore()
+    for hop in range(1, peers):
+        pl.semaphore_signal(
+            barrier,
+            inc=1,
+            device_id={"req": lax.rem(me + hop, peers)},
+            device_id_type=pl.DeviceIdType.MESH,
         )
-        pltpu.make_async_copy(pool.at[page], out.at[target, number], sem).start()
+    pl.semaphore_wait(barrier, peers - 1)
+    copies = []
+    for hop in range(1, peers):
+        copy = pltpu.make_async_remote_copy(
+            src_ref=mine,
+            dst_ref=out.at[me],
+            send_sem=send_sems.at[hop - 1],
+            recv_sem=recv_sems.at[hop - 1],
+            device_id={"req": lax.rem(me + hop, peers)},
+            device_id_type=pl.DeviceIdType.MESH,
+        )
+        copy.start()
+        copies.append(copy)
+    out[me] = mine[...]
+    for copy in copies:
+        copy.wait()
+
+
+def exchange(peers, mine):
+    return pl.pallas_call(
+        lambda *refs: exchange_kernel(peers, *refs),
+        out_shape=jax.ShapeDtypeStruct((peers,) + mine.shape, mine.dtype),
+        in_specs=[pl.BlockSpec(memory_space=pltpu.VMEM)],
+        out_specs=pl.BlockSpec(memory_space=pltpu.VMEM),
+        scratch_shapes=[
+            pltpu.SemaphoreType.DMA((peers - 1,)),
+            pltpu.SemaphoreType.DMA((peers - 1,)),
+        ],
+        compiler_params=pltpu.CompilerParams(collective_id=0, has_side_effects=True),
+        name="exchange",
+    )(mine)
+
+
+BUFFERS = 16
+AHEAD = 8
+
+
+def ring(count, load, store, drain):
+    def step(index, carry):
+        @pl.when(index < count)
+        def _():
+            @pl.when(index >= BUFFERS)
+            def _():
+                drain(index - BUFFERS)
+
+            load(index)
+
+        @pl.when(index >= AHEAD)
+        def _():
+            store(index - AHEAD)
+
         return carry
 
-    lax.fori_loop(0, layout.peers * layout.block, send, 0)
-    pltpu.make_async_copy(out, out, sem).wait()
-
-
-def pack_pages(layout, table, perm, me, pool):
+    lax.fori_loop(0, count + AHEAD, step, 0)
+
+    def last(index, carry):
+        drain(index)
+        return carry
+
+    lax.fori_loop(max(count - BUFFERS, 0), count, last, 0)
+
+
+def copy_rows(source, source_row, target, target_row, count, sem):
+    size = target.shape[0]
+    while size:
+        offset = lax.div(count, 2 * size) * (2 * size)
+
+        @pl.when(lax.rem(lax.div(count, size), 2) == 1)
+        def _(size=size, offset=offset):
+            pltpu.make_async_copy(
+                source.at[pl.ds(source_row + offset, size)],
+                target.at[pl.ds(target_row + offset, size)],
+                sem,
+            ).start()
+
+        size //= 2
+
+
+def pack_kernel(layout, late, table, perm, me, pool, *rest):
+    if late:
+        recent, zeros, out, codes, buffers, in_sems, out_sems = rest
+    else:
+        out, codes, buffers, in_sems, out_sems = rest
+    page_len = buffers.shape[1]
+    span = layout.late if late else layout.early
+    start = layout.early if late else 0
+    count = layout.peers * span
+
+    def clear(index, carry):
+        codes[index] = 0
+        return carry
+
+    lax.fori_loop(0, layout.peers * layout.block, clear, 0)
+
+    def block(target, carry):
+        def use(number, code, place):
+            @pl.when(place >= 0)
+            def _():
+                codes[target * layout.block + place] = code
+
+        layout.visit(table, perm, me[0], target, page_len, use)
+        return carry
+
+    lax.fori_loop(0, layout.peers, block, 0)
+
+    def load(index):
+        spot = lax.rem(index, BUFFERS)
+        code = codes[lax.div(index, span) * layout.block + start + lax.rem(index, span)]
+        slot, page = layout.split(code)
+        cached = pool.at[layout.physical(table, perm, me[0], slot, page)]
+        target, sem = buffers.at[spot], in_sems.at[spot]
+        if not late:
+            pltpu.make_async_copy(cached, target, sem).start()
+            return
+        length = layout.length(table, perm, me[0], slot)
+        full, kept = lax.div(length, page_len), lax.rem(length, page_len)
+
+        @pl.when(page < full)
+        def _():
+            pltpu.make_async_copy(cached, target, sem).start()
+
+        @pl.when(page == full)
+        def _():
+            copy_rows(cached, 0, target, 0, kept, sem)
+            copy_rows(recent.at[slot], 0, target, kept, page_len - kept, sem)
+
+        @pl.when(page > full)
+        def _():
+            copy_rows(recent.at[slot], page_len - kept, target, 0, kept, sem)
+            copy_rows(zeros, 0, target, kept, page_len - kept, sem)
+
+    def outward(index):
+        spot = lax.rem(index, BUFFERS)
+        target = out.at[lax.div(index, span), lax.rem(index, span)]
+        return pltpu.make_async_copy(buffers.at[spot], target, out_sems.at[spot])
+
+    def store(index):
+        spot = lax.rem(index, BUFFERS)
+        pltpu.make_async_copy(pool.at[0], buffers.at[spot], in_sems.at[spot]).wait()
+        outward(index).start()
+
+    ring(count, load, store, lambda index: outward(index).wait())
+
+
+def scratch(layout, pool):
+    return [
+        pltpu.SMEM((layout.peers * layout.block,), jnp.int32),
+        pltpu.VMEM((BUFFERS,) + pool.shape[-3:], pool.dtype),
+        pltpu.SemaphoreType.DMA((BUFFERS,)),
+        pltpu.SemaphoreType.DMA((BUFFERS,)),
+    ]
+
+
+def pack_pages(layout, table, perm, me, pool, *fresh):
+    late = bool(fresh)
+    span = layout.late if late else layout.early
     return pl.pallas_call(
-        lambda *refs: pack_kernel(layout, *refs),
-        out_shape=jax.ShapeDtypeStruct((layout.peers, layout.block) + pool.shape[1:], pool.dtype),
+        lambda *refs: pack_kernel(layout, late, *refs),
+        out_shape=jax.ShapeDtypeStruct((layout.peers, span) + pool.shape[1:], pool.dtype),
         grid_spec=pltpu.PrefetchScalarGridSpec(
             num_scalar_prefetch=3,
             grid=(1,),
-            in_specs=[pl.BlockSpec(memory_space=pl.ANY)],
+            in_specs=[pl.BlockSpec(memory_space=pl.ANY)] * (1 + len(fresh)),
             out_specs=pl.BlockSpec(memory_space=pl.ANY),
-            scratch_shapes=[pltpu.SemaphoreType.DMA],
+            scratch_shapes=scratch(layout, pool),
         ),
-        name="pack_pages",
-    )(table, perm, me, pool)
-
-
-def finish_kernel(layout, table, perm, me, arrived, recent, zeros, out, sem):
-    page_len = out.shape[2]
-
-    def rows(source, source_row, target, target_row, count):
-        size = page_len
-        while size:
-            offset = count // (2 * size) * (2 * size)
-
-            @pl.when(count // size % 2 == 1)
-            def _(size=size, offset=offset):
-                pltpu.make_async_copy(
-                    source.at[pl.ds(source_row + offset, size)],
-                    target.at[pl.ds(target_row + offset, size)],
-                    sem,
-                ).start()
-
-            size //= 2
-
-    def place(index, carry):
-        source, number = index // layout.block, index % layout.block
-        raw_code = layout.code(table, source, me[0], number)
-        code = jnp.maximum(raw_code, 0)
-        slot, page = code // layout.code_width, code % layout.code_width
-        length = layout.length(table, perm, source, slot)
-        full, kept = length // page_len, length % page_len
-        target = out.at[source, number]
-        valid = raw_code >= 0
-
-        @pl.when(valid & (page < full))
-        def _():
-            pltpu.make_async_copy(arrived.at[source, number], target, sem).start()
-
-        @pl.when(jnp.logical_not(valid) | (page > full + 1))
-        def _():
-            pltpu.make_async_copy(zeros, target, sem).start()
-
-        @pl.when(valid & (page == full))
-        def _():
-            rows(arrived.at[source, number], 0, target, 0, kept)
-            rows(recent.at[source, slot], 0, target, kept, page_len - kept)
-
-        @pl.when(valid & (page == full + 1))
-        def _():
-            rows(recent.at[source, slot], page_len - kept, target, 0, kept)
-            rows(zeros, 0, target, kept, page_len - kept)
-
+        name="pack_late" if late else "pack_early",
+    )(table, perm, me, pool, *fresh)
+
+
+def place_kernel(layout, table, perm, me, arrived, zeros, out, places, buffers, in_sems, out_sems, blank, blank_sem):
+    page_len = buffers.shape[1]
+    fill = pltpu.make_async_copy(zeros, blank, blank_sem)
+    fill.start()
+
+    def block(source, carry):
+        def use(number, code, place):
+            places[source * layout.block + number] = place
+
+        layout.visit(table, perm, source, me[0], page_len, use)
         return carry
 
-    lax.fori_loop(0, layout.peers * layout.block, place, 0)
-    pltpu.make_async_copy(out, out, sem).wait()
-
-
-def finish_pages(layout, table, perm, me, arrived, recent):
-    zeros = jnp.zeros(arrived.shape[2:], arrived.dtype)
+    lax.fori_loop(0, layout.peers, block, 0)
+    fill.wait()
+
+    def inward(index):
+        spot = lax.rem(index, BUFFERS)
+        place = jnp.clip(places[index], 0, layout.early - 1)
+        return pltpu.make_async_copy(
+            arrived.at[lax.div(index, layout.block), place], buffers.at[spot], in_sems.at[spot]
+        )
+
+    def outward(index, held):
+        target = out.at[lax.div(index, layout.block), lax.rem(index, layout.block)]
+        return pltpu.make_async_copy(held, target, out_sems.at[lax.rem(index, BUFFERS)])
+
+    def is_early(index):
+        return (places[index] >= 0) & (places[index] < layout.early)
+
+    def load(index):
+        @pl.when(is_early(index))
+        def _():
+            inward(index).start()
+
+    def store(index):
+        @pl.when(is_early(index))
+        def _():
+            inward(index).wait()
+            outward(index, buffers.at[lax.rem(index, BUFFERS)]).start()
+
+        @pl.when(places[index] < 0)
+        def _():
+            outward(index, blank).start()
+
+    def drain(index):
+        @pl.when(places[index] < layout.early)
+        def _():
+            outward(index, blank).wait()
+
+    ring(layout.peers * layout.block, load, store, drain)
+
+
+def place_late_kernel(layout, table, perm, me, arrived, held, out, numbers, buffers, in_sems, out_sems):
+    page_len = buffers.shape[1]
+
+    def clear(index, carry):
+        numbers[index] = -1
+        return carry
+
+    lax.fori_loop(0, layout.peers * layout.late, clear, 0)
+
+    def block(source, carry):
+        def use(number, code, place):
+            @pl.when(place >= layout.early)
+            def _():
+                numbers[source * layout.late + place - layout.early] = number
+
+        layout.visit(table, perm, source, me[0], page_len, use)
+        return carry
+
+    lax.fori_loop(0, layout.peers, block, 0)
+
+    def inward(index):
+        spot = lax.rem(index, BUFFERS)
+        return pltpu.make_async_copy(
+            arrived.at[lax.div(index, layout.late), lax.rem(index, layout.late)],
+            buffers.at[spot],
+            in_sems.at[spot],
+        )
+
+    def outward(index):
+        spot = lax.rem(index, BUFFERS)
+        target = out.at[lax.div(index, layout.late), jnp.maximum(numbers[index], 0)]
+        return pltpu.make_async_copy(buffers.at[spot], target, out_sems.at[spot])
+
+    def load(index):
+        @pl.when(numbers[index] >= 0)
+        def _():
+            inward(index).start()
+
+    def store(index):
+        @pl.when(numbers[index] >= 0)
+        def _():
+            inward(index).wait()
+            outward(index).start()
+
+    def drain(index):
+        @pl.when(numbers[index] >= 0)
+        def _():
+            outward(index).wait()
+
+    ring(layout.peers * layout.late, load, store, drain)
+
+
+def place_early_pages(layout, table, perm, me, arrived, zeros):
+    page = arrived.shape[2:]
     return pl.pallas_call(
-        lambda *refs: finish_kernel(layout, *refs),
-        out_shape=jax.ShapeDtypeStruct(arrived.shape, arrived.dtype),
+        lambda *refs: place_kernel(layout, *refs),
+        out_shape=jax.ShapeDtypeStruct((layout.peers, layout.block) + page, arrived.dtype),
         grid_spec=pltpu.PrefetchScalarGridSpec(
             num_scalar_prefetch=3,
             grid=(1,),
-            in_specs=[pl.BlockSpec(memory_space=pl.ANY)] * 3,
+            in_specs=[pl.BlockSpec(memory_space=pl.ANY)] * 2,
             out_specs=pl.BlockSpec(memory_space=pl.ANY),
-            scratch_shapes=[pltpu.SemaphoreType.DMA],
+            scratch_shapes=scratch(layout, arrived)
+            + [pltpu.VMEM(page, arrived.dtype), pltpu.SemaphoreType.DMA],
         ),
-        name="finish_pages",
-    )(table, perm, me, arrived, recent, zeros)
+        name="place_early",
+    )(table, perm, me, arrived, zeros)
+
+
+def place_late_pages(layout, table, perm, me, arrived, held):
+    return pl.pallas_call(
+        lambda *refs: place_late_kernel(layout, *refs),
+        out_shape=jax.ShapeDtypeStruct(held.shape, held.dtype),
+        grid_spec=pltpu.PrefetchScalarGridSpec(
+            num_scalar_prefetch=3,
+            grid=(1,),
+            in_specs=[pl.BlockSpec(memory_space=pl.ANY)] * 2,
+            out_specs=pl.BlockSpec(memory_space=pl.ANY),
+            scratch_shapes=scratch(layout, arrived),
+        ),
+        input_output_aliases={4: 0},
+        name="place_late",
+    )(table, perm, me, arrived, held)
 
 
 def attend_kernel(lengths, tables, q_ref, nk_ref, nv_ref, *rest):
@@ -292,14 +539,16 @@
     device = lax.axis_index("req")
     me = device.astype(jnp.int32).reshape(1)
     mine = jnp.concatenate([prior_len, page_table.reshape(-1), send_table.reshape(-1)])
-    table = lax.all_gather(mine, "req", axis=0, tiled=True)
+    mine = jnp.pad(mine, (0, layout.width - layout.used)).reshape(-1, 128)
+    by_device = exchange(peers, mine)
+    table = by_device.reshape(-1)
+    by_device = by_device.reshape(peers, layout.width)
     outgoing = pack_pages(layout, table, perm, me, pool)
     arrived = lax.all_to_all(outgoing, "req", split_axis=0, concat_axis=0, tiled=True)
 
     full_rows = lax.all_gather(hidden, "tp", axis=1, tiled=True)
     late_pool, wkv, outgoing = lax.optimization_barrier((pool, wkv, outgoing))
     requests = lax.dynamic_slice_in_dim(perm, device * slots, slots)
-    by_device = table.reshape(peers, layout.width)
     lengths = by_device[:, :slots].reshape(-1)[requests]
     tables = by_device[:, slots : layout.sends].reshape(-1, layout.row_pages)[requests]
 
@@ -316,8 +565,6 @@
     new_keys = rotate(pair_heads[:, 0], positions).astype(jnp.bfloat16).reshape(-1, features)
     new_values = pair_heads[:, 1].astype(jnp.bfloat16).reshape(-1, features)
     recent = jnp.stack([new_keys, new_values], axis=1).reshape(slots, tokens, 2, features)
-    all_recent = lax.all_gather(recent, "req", axis=0)
-
     context = attend(
         lengths,
         tables,
@@ -328,10 +575,20 @@
         late_pool[:, :, 1],
     )
     partial_value = jnp.dot(context, wo, preferred_element_type=jnp.float32)
+    recent, partial_value = lax.optimization_barrier((recent, partial_value))
     attn_out = lax.psum_scatter(
         partial_value.astype(jnp.bfloat16), "tp", scatter_dimension=1, tiled=True
     )
-    decode_pages = finish_pages(layout, table, perm, me, arrived, all_recent)
+    zeros = jnp.zeros(pool.shape[1:], pool.dtype)
+    late_arrived = lax.all_to_all(
+        pack_pages(layout, table, perm, me, late_pool, recent, zeros),
+        "req",
+        split_axis=0,
+        concat_axis=0,
+        tiled=True,
+    )
+    early_pages = place_early_pages(layout, table, perm, me, arrived, zeros)
+    decode_pages = place_late_pages(layout, table, perm, me, late_arrived, early_pages)
     return (attn_out, decode_pages[None])
 
 

time: 1550 us -> 454 us (0.29)
  Pallas kernels: 1130 us -> 118 us
  blocking collectives: 38.8 us -> 0 us
  waiting for transfers between devices: 278 us -> 243 us
    pallas_call x2 -> x5, Pallas kernels: 1080 us -> 66.8 us  [the longest x2 29.9 us: pack_pages(): pl.pallas_call(lambda *refs: pack_kernel(layout, late, *refs), out_shape=...]
    all_gather x1 -> x0, waiting for transfers between devices: 197 us -> none  [shards(): all_recent = lax.all_gather(recent, 'req', axis=0)]
    all_to_all x1, waiting for transfers between devices: 80.4 us -> 168 us  [shards(): lax.all_to_all(outgoing, 'req', split_axis=0, concat_axis=0, tiled=True)]
    all_to_all x0 -> x1, waiting for transfers between devices: none -> 73.5 us  [shards(): lax.all_to_all(pack_pages(layout, table, perm, me, late_pool, recent, zer...]
    unnamed x1 -> x0, blocking collectives: 38.8 us -> none
  transfers between devices with their start and end apart: 4 -> 4, of which waited for: 2 -> 2; matrix products, arithmetic and copies ran while one was open for 5% -> 13% of each run, Pallas kernels for 38% -> 20%
where the time goes in v1:
time: 454 us; the launch traced here: 453 us
  waiting for transfers between devices  243 us (54%)
  Pallas kernels  118 us (26%)
  local copies, waits for them, and re-layouts  41.9 us (9%)
  matrix products  19 us (4%)
  between operations  14.4 us (3%)
  starting transfers between devices  10.1 us (2%)
  other arithmetic  5.73 us (1%)
    all_to_all x1, waiting for transfers between devices, shards(): lax.all_to_all(outgoing, 'req', split_axis=0, concat_axis=0, tiled=True)  168 us
    all_to_all x1, waiting for transfers between devices, shards(): lax.all_to_all(pack_pages(layout, table, perm, me, late_pool, recent, zer...  73.5 us
    pallas_call x1, Pallas kernels, attend(): pl.pallas_call(attend_kernel, out_shape=jax.ShapeDtypeStruct(queries.shap...  51.3 us
    pallas_call x2, Pallas kernels, pack_pages(): pl.pallas_call(lambda *refs: pack_kernel(layout, late, *refs), out_shape=...  29.9 us
    pallas_call x1, Pallas kernels, place_early_pages(): pl.pallas_call(lambda *refs: place_kernel(layout, *refs), out_shape=jax.S...  18.3 us
    unnamed x22, local copies, waits for them, and re-layouts  10.1 us
    optimization_barrier x1, local copies, waits for them, and re-layouts, shards(): late_pool, wkv, outgoing = lax.optimization_barrier((pool, wkv, outgoing))  9.98 us
    pallas_call x1, Pallas kernels, exchange(): pl.pallas_call(lambda *refs: exchange_kernel(peers, *refs), out_shape=jax...  9.75 us
  transfers between devices with their start and end apart: 4, of which 2 were waited for; matrix products, arithmetic and copies ran while one was open for 13% of the time, Pallas kernels for 20%

profile of v1, /device:TPU:0, one launch (start us, length us, event | category | flops | bytes accessed | tf_op | source)
XLA Modules:
  0.0 452.6 jit_solution(13035291702192399324)
XLA Ops:
  7.2 0.8 reshape.153
  7.9 0.8 reshape.152
  8.7 0.7 pad_add_fusion
  9.4 0.6 pad_bitcast_fusion.refs_0_
  10.0 9.7 %exchange.1 = s32[8,8,128]{2,1,0:T(8,128)} custom-call(s32[8,128]{1,0:T(8,128)} %pad_bitcast_fusion.refs_0_), custom_call_target="tpu_custom_call" | custom-call | tf_op jit(solution)/shard_map/exchange/pallas_call | solution.py:122
  19.8 19.6 %pack_early.1 = bf16[8,13,128,2,256]{4,3,2,1,0:T(2,128)(2,1)} custom-call(s32[8192]{0:T(1024)} %bitcast.55, s32[16]{0:T(128)} %refs_1_.7, s32[1]{0:T(128)} %bitcast.4.refs_2_, bf16[128,128,2,256]{3,2,1,0:T(2,128)(2,1)} %refs_3_.2), custom_call_target="tpu_custom_call" | custom-call | tf_op jit(solution)/shard_map/pack_early/pallas_call | solution.py:259
  39.4 5.5 %all-to-all-start.1 = ((bf16[8,13,128,2,256]{4,3,2,1,0:T(2,128)(2,1)}), bf16[8,13,128,2,256]{4,3,2,1,0:T(2,128)(2,1)}, u32[]{:S(2)}, u32[]{:S(2)}) async-start(bf16[8,13,128,2,256]{4,3,2,1,0:T(2,128)(2,1)} %pack_early.1), calls=%async_computation.2 | async-start | bytes 27262976 | tf_op jit(solution)/shard_map/all_to_all | solution.py:547
  44.9 0.7 all-gather.2.cloned.1.call-update
  45.7 5.6 %copy.40 = bf16[640,8,2,256]{3,1,2,0:T(8,128)(2,1)} copy(bf16[640,8,2,256]{3,2,1,0:T(2,128)(2,1)} %bitcast.50) | data formatting | bytes 10485760
  51.4 7.9 %copy.22 = bf16[512,5120]{1,0:T(8,128)(2,1)} copy(bf16[512,5120]{0,1:T(8,128)(2,1)} %bitcast.48) | data formatting | bytes 10485760 | tf_op jit(solution)/shard_map/dot_general | solution.py:557
  59.5 0.6 gather_fusion
  61.2 0.8 copy.28
  62.0 0.8 copy.27
  62.7 10.0 %copy.31 = bf16[128,128,2,256]{3,1,0,2:T(8,128)(2,1)S(1)} copy(bf16[128,128,2,256]{3,2,1,0:T(2,128)(2,1)} %refs_3_.2) | data formatting | bytes 33554432 | tf_op jit(solution)/shard_map/optimization_barrier | solution.py:550
  72.7 6.4 %slice_bitcast_fusion = (bf16[128,128,256]{2,1,0:T(8,128)(2,1)}, bf16[128,128,256]{2,1,0:T(8,128)(2,1)}) fusion(bf16[128,128,2,256]{3,1,0,2:T(8,128)(2,1)S(1)} %copy.31), kind=kLoop, calls=%fused_computation.2 | loop fusion | bytes 33554432 | tf_op jit(solution)/shard_map/squeeze | solution.py:575
  79.1 2.3 fusion
  81.5 5.1 %fusion.3 = f32[256,2,2,128]{0,3,2,1:T(8,128)S(1)} fusion(bf16[2,2,128,5120]{3,2,1,0:T(8,128)(2,1)} %bitcast.51, bf16[256,5120]{1,0:T(8,128)(2,1)} %all-gather.2.cloned.1.call-done, f32[5120]{0:T(1024)S(1)} %convert_element_type.65, f32[256]{0:T(256)S(1)} %add_rsqrt_fusion), kind=kOutput, calls=%fused_computation.9 | convolution fusion | flops 1347420160 | bytes 8410112 | tf_op jit(solution)/shard_map/dot_general | solution.py:557
  86.5 0.8 copy-done.5
  87.6 1.0 slice_bitcast_fusion.2
  88.9 5.8 %convolution_bitcast_fusion = f32[32,8,8,128]{3,1,2,0:T(8,128)S(1)} fusion(bf16[5120,1024]{1,0:T(8,128)(2,1)} %param.12, bf16[256,5120]{1,0:T(8,128)(2,1)S(1)} %copy-done.1, f32[5120]{0:T(1024)} %copy-done.6, f32[256]{0:T(256)S(1)} %add_rsqrt_fusion), kind=kOutput, calls=%fused_computation.11 | convolution fusion | flops 2689597440 | bytes 14177280 | tf_op jit(solution)/shard_map/dot_general | solution.py:556
  96.1 3.4 copy-done
  99.5 51.3 %attend.1 = bf16[256,1024]{1,0:T(8,128)(2,1)S(1)} custom-call(s32[2]{0:T(128)S(1)} %gather_fusion, s32[128]{0:T(128)S(1)} %reshape.161.tables, bf16[256,1024]{1,0:T(8,128)(2,1)S(1)} %bitcast.46, bf16[256,256]{1,0:T(8,128)(2,1)S(1)} %copy.38.nk_ref, bf16[256,256]{1,0:T(8,128)(2,1)S(1)} %copy.39.nv_ref, bf16[128,128,256]{2,1,0:T(8,128)(2,1)S(1)} %copy-done, ...), custom_call_target="tpu_custom_call" | custom-call | tf_op jit(solution)/shard_map/attend/pallas_call | solution.py:497
  150.8 1.3 pad_maximum_fusion.1.refs_4_
  152.1 8.1 %fusion.7 = bf16[256,5120]{1,0:T(8,128)(2,1)} fusion(bf16[256,1024]{1,0:T(8,128)(2,1)S(1)} %attend.1, bf16[1024,5120]{1,0:T(8,128)(2,1)} %param.14), kind=kOutput, calls=%fused_computation.32 | convolution fusion | flops 2684354560 | bytes 13631488 | tf_op jit(solution)/shard_map/dot_general | solution.py:577
  160.2 0.7 broadcast_in_dim.7.refs_5_.refs_4_
  160.9 10.3 %pack_late.1 = bf16[8,4,128,2,256]{4,3,2,1,0:T(2,128)(2,1)} custom-call(s32[8192]{0:T(1024)} %bitcast.56, s32[16]{0:T(128)} %refs_1_.7, s32[1]{0:T(128)} %bitcast.4.refs_2_, bf16[128,128,2,256]{3,2,1,0:T(2,128)(2,1)} %refs_3_.2, bf16[2,128,2,256]{3,2,1,0:T(2,128)(2,1)} %pad_maximum_fusion.1.refs_4_, bf16[128,2,256]{2,1,0:T(2,128)(2,1)} %broadcast_in_dim.7.refs_5_.refs_4_), custom_call_target="tpu_custom_call" | custom-call | tf_op jit(solution)/shard_map/pack_late/pallas_call | solution.py:259
  171.2 168.5 %all-to-all-done.1.refs_3_ = bf16[8,13,128,2,256]{4,3,2,1,0:T(2,128)(2,1)} async-done(((bf16[8,13,128,2,256]{4,3,2,1,0:T(2,128)(2,1)}), bf16[8,13,128,2,256]{4,3,2,1,0:T(2,128)(2,1)}, u32[]{:S(2)}, u32[]{:S(2)}) %all-to-all-start.1) | async-done | bytes 13631520 | tf_op jit(solution)/shard_map/all_to_all | solution.py:547
  339.7 4.6 %all-to-all-start = ((bf16[8,4,128,2,256]{4,3,2,1,0:T(2,128)(2,1)}), bf16[8,4,128,2,256]{4,3,2,1,0:T(2,128)(2,1)}, u32[]{:S(2)}, u32[]{:S(2)}) async-start(bf16[8,4,128,2,256]{4,3,2,1,0:T(2,128)(2,1)} %pack_late.1), calls=%async_computation.1 | async-start | bytes 8388608 | tf_op jit(solution)/shard_map/all_to_all | solution.py:583
  344.3 0.7 reduce-scatter.2.cloned.1.call-update
  345.0 18.3 %place_early.1.refs_4_ = bf16[8,17,128,2,256]{4,3,2,1,0:T(2,128)(2,1)} custom-call(s32[8192]{0:T(1024)} %bitcast.57, s32[16]{0:T(128)} %refs_1_.7, s32[1]{0:T(128)} %bitcast.4.refs_2_, bf16[8,13,128,2,256]{4,3,2,1,0:T(2,128)(2,1)} %all-to-all-done.1.refs_3_, bf16[128,2,256]{2,1,0:T(2,128)(2,1)} %broadcast_in_dim.7.refs_5_.refs_4_), custom_call_target="tpu_custom_call" | custom-call | tf_op jit(solution)/shard_map/place_early/pallas_call | solution.py:379
  363.3 73.5 %all-to-all-done.refs_3_ = bf16[8,4,128,2,256]{4,3,2,1,0:T(2,128)(2,1)} async-done(((bf16[8,4,128,2,256]{4,3,2,1,0:T(2,128)(2,1)}), bf16[8,4,128,2,256]{4,3,2,1,0:T(2,128)(2,1)}, u32[]{:S(2)}, u32[]{:S(2)}) %all-to-all-start) | async-done | bytes 4194336 | tf_op jit(solution)/shard_map/all_to_all | solution.py:583
  436.8 8.9 %place_late.1 = bf16[8,17,128,2,256]{4,3,2,1,0:T(2,128)(2,1)} custom-call(s32[8192]{0:T(1024)} %bitcast.58, s32[16]{0:T(128)} %refs_1_.7, s32[1]{0:T(128)} %bitcast.4.refs_2_, bf16[8,4,128,2,256]{4,3,2,1,0:T(2,128)(2,1)} %all-to-all-done.refs_3_, bf16[8,17,128,2,256]{4,3,2,1,0:T(2,128)(2,1)} %place_early.1.refs_4_), custom_call_target="tpu_custom_call", output_to_operand_aliasing={{}: (4, {})} | custom-call | tf_op jit(solution)/shard_map/place_late/pallas_call | solution.py:395
  (47 shorter events, 3.3 us)
Async XLA Ops:
  39.4 6.2 %copy-start.2 = (s32[8,8,128]{2,1,0:T(8,128)S(1)}, s32[8,8,128]{2,1,0:T(8,128)}, u32[]{:S(2)}) copy-start(s32[8,8,128]{2,1,0:T(8,128)} %exchange.1) | copy-start | bytes 98308
  39.4 300.3 %all-to-all-start.1 = ((bf16[8,13,128,2,256]{4,3,2,1,0:T(2,128)(2,1)}), bf16[8,13,128,2,256]{4,3,2,1,0:T(2,128)(2,1)}, u32[]{:S(2)}, u32[]{:S(2)}) async-start(bf16[8,13,128,2,256]{4,3,2,1,0:T(2,128)(2,1)} %pack_early.1), calls=%async_computation.2 | async-start | bytes 27262976 | tf_op jit(solution)/shard_map/all_to_all | solution.py:547
  44.9 34.2 %all-gather.2.cloned.1.call-start = ((), (), s32[]{:S(2)}) async-start(), calls=%async_computation.3 | async-start | bytes 3276800 | tf_op jit(solution)/shard_map/all_gather | solution.py:549
  51.4 7.9 %copy-start.7 = (bf16[5120]{0:T(1024)(128)(2,1)S(1)}, bf16[5120]{0:T(1024)(128)(2,1)}, u32[]{:S(2)}) copy-start(bf16[5120]{0:T(1024)(128)(2,1)} %param.11) | copy-start | bytes 30724
  51.4 8.1 %copy-start.8 = (s32[16]{0:T(128)S(1)}, s32[16]{0:T(128)}, u32[]{:S(2)}) copy-start(s32[16]{0:T(128)} %refs_1_.7) | copy-start | bytes 196
  59.3 22.2 %copy-start.6 = (f32[5120]{0:T(1024)}, f32[5120]{0:T(1024)S(1)}, u32[]{:S(2)}) copy-start(f32[5120]{0:T(1024)S(1)} %convert_element_type.65) | copy-start | bytes 61444
  81.4 7.4 %copy-start.1 = (bf16[256,5120]{1,0:T(8,128)(2,1)S(1)}, bf16[256,5120]{1,0:T(8,128)(2,1)}, u32[]{:S(2)}) copy-start(bf16[256,5120]{1,0:T(8,128)(2,1)} %all-gather.2.cloned.1.call-done) | copy-start | bytes 7864324
  86.5 0.8 copy-start.5
  88.9 6.0 %copy-start.3 = (f32[256,64]{1,0:T(8,128)S(1)}, f32[256,64]{1,0:T(8,128)}, u32[]{:S(2)}) copy-start(f32[256,64]{1,0:T(8,128)} %copy.28) | copy-start | bytes 196612
  88.9 6.0 %copy-start.4 = (f32[256,64]{1,0:T(8,128)S(1)}, f32[256,64]{1,0:T(8,128)}, u32[]{:S(2)}) copy-start(f32[256,64]{1,0:T(8,128)} %copy.27) | copy-start | bytes 196612
  96.1 3.4 copy-start
  339.7 97.1 %all-to-all-start = ((bf16[8,4,128,2,256]{4,3,2,1,0:T(2,128)(2,1)}), bf16[8,4,128,2,256]{4,3,2,1,0:T(2,128)(2,1)}, u32[]{:S(2)}, u32[]{:S(2)}) async-start(bf16[8,4,128,2,256]{4,3,2,1,0:T(2,128)(2,1)} %pack_late.1), calls=%async_computation.1 | async-start | bytes 8388608 | tf_op jit(solution)/shard_map/all_to_all | solution.py:583
  344.3 101.5 %reduce-scatter.2.cloned.1.call-start = ((), (), s32[]{:S(2)}) async-start(), calls=%async_computation.4 | async-start | bytes 3276800 | tf_op jit(solution)/shard_map/reduce_scatter | solution.py:579
Sparse Core Ops, SparseCore 0:
  47.3 26.8 all-gather.1
  348.2 35.9 reduce-scatter.1

commit v2 on v1

--- a/solution.py
+++ b/solution.py
@@ -70,24 +70,18 @@
             lax.div(self.length(table, perm, source, slot), page_len) for slot in range(self.slots)
         ]
         base = source * self.width + self.sends + target * self.block
-
-        def step(number, counts):
-            plain, tails = counts
+        plain, tails = jnp.int32(0), jnp.int32(self.block - 1)
+        for number in range(self.block):
             code = table[base + number]
-            valid = code >= 0
-            slot, page = self.split(jnp.maximum(code, 0))
             first = whole[0]
-            for other in range(1, self.slots):
-                first = jnp.where(slot == other, whole[other], first)
-            tail = valid & (page >= first)
-            place = jnp.where(valid, jnp.where(tail, self.block - 1 - tails, plain), -1)
+            for slot in range(1, self.slots):
+                low = slot * self.code_width
+                first = jnp.where(code >= low, whole[slot] + low, first)
+            valid, tail = code >= 0, code >= first
+            place = jnp.where(valid, jnp.where(tail, tails, plain), -1)
             use(number, code, place)
-            return (
-                plain + jnp.where(valid & jnp.logical_not(tail), 1, 0),
-                tails + jnp.where(tail, 1, 0),
-            )
-
-        lax.fori_loop(0, self.block, step, (jnp.int32(0), jnp.int32(0)))
+            plain = plain + jnp.where(valid & jnp.logical_not(tail), 1, 0)
+            tails = tails - jnp.where(tail, 1, 0)
 
 
 def exchange_kernel(peers, mine, out, send_sems, recv_sems):
@@ -133,8 +127,8 @@
     )(mine)
 
 
-BUFFERS = 16
-AHEAD = 8
+BUFFERS = 32
+AHEAD = 16
 
 
 def ring(count, load, store, drain):
@@ -192,13 +186,27 @@
         codes[index] = 0
         return carry
 
-    lax.fori_loop(0, layout.peers * layout.block, clear, 0)
+    lax.fori_loop(0, count, clear, 0)
+    starts = []
+    for slot in range(layout.slots):
+        base, row = layout.request(perm, me[0], slot)
+        starts.append(
+            base + layout.slots + row * layout.row_pages - slot * layout.code_width
+        )
 
     def block(target, carry):
         def use(number, code, place):
-            @pl.when(place >= 0)
+            inside = (place >= start) & (place < start + span)
+            item = code
+            if not late:
+                origin = starts[0]
+                for slot in range(1, layout.slots):
+                    origin = jnp.where(code >= slot * layout.code_width, starts[slot], origin)
+                item = table[jnp.where(inside, origin + code, 0)]
+
+            @pl.when(inside)
             def _():
-                codes[target * layout.block + place] = code
+                codes[target * span + place - start] = item
 
         layout.visit(table, perm, me[0], target, page_len, use)
         return carry
@@ -206,14 +214,13 @@
     lax.fori_loop(0, layout.peers, block, 0)
 
     def load(index):
-        spot = lax.rem(index, BUFFERS)
-        code = codes[lax.div(index, span) * layout.block + start + lax.rem(index, span)]
-        slot, page = layout.split(code)
-        cached = pool.at[layout.physical(table, perm, me[0], slot, page)]
+        spot = index & (BUFFERS - 1)
         target, sem = buffers.at[spot], in_sems.at[spot]
         if not late:
-            pltpu.make_async_copy(cached, target, sem).start()
+            pltpu.make_async_copy(pool.at[codes[index]], target, sem).start()
             return
+        slot, page = layout.split(codes[index])
+        cached = pool.at[layout.physical(table, perm, me[0], slot, page)]
         length = layout.length(table, perm, me[0], slot)
         full, kept = lax.div(length, page_len), lax.rem(length, page_len)
 
@@ -232,12 +239,11 @@
             copy_rows(zeros, 0, target, kept, page_len - kept, sem)
 
     def outward(index):
-        spot = lax.rem(index, BUFFERS)
-        target = out.at[lax.div(index, span), lax.rem(index, span)]
-        return pltpu.make_async_copy(buffers.at[spot], target, out_sems.at[spot])
+        spot = index & (BUFFERS - 1)
+        return pltpu.make_async_copy(buffers.at[spot], out.at[index], out_sems.at[spot])
 
     def store(index):
-        spot = lax.rem(index, BUFFERS)
+        spot = index & (BUFFERS - 1)
         pltpu.make_async_copy(pool.at[0], buffers.at[spot], in_sems.at[spot]).wait()
         outward(index).start()
 
@@ -258,7 +264,7 @@
     span = layout.late if late else layout.early
     return pl.pallas_call(
         lambda *refs: pack_kernel(layout, late, *refs),
-        out_shape=jax.ShapeDtypeStruct((layout.peers, span) + pool.shape[1:], pool.dtype),
+        out_shape=jax.ShapeDtypeStruct((layout.peers * span,) + pool.shape[1:], pool.dtype),
         grid_spec=pltpu.PrefetchScalarGridSpec(
             num_scalar_prefetch=3,
             grid=(1,),
@@ -267,11 +273,18 @@
             scratch_shapes=scratch(layout, pool),
         ),
         name="pack_late" if late else "pack_early",
-    )(table, perm, me, pool, *fresh)
-
-
-def place_kernel(layout, table, perm, me, arrived, zeros, out, places, buffers, in_sems, out_sems, blank, blank_sem):
+    )(table, perm, me, pool, *fresh).reshape((layout.peers, span) + pool.shape[1:])
+
+
+def place_kernel(layout, table, perm, me, arrived, zeros, *rest):
+    out, numbers, places, buffers, in_sems, out_sems, blank, blank_sem = rest
     page_len = buffers.shape[1]
+
+    def clear(index, carry):
+        numbers[index] = -1
+        return carry
+
+    lax.fori_loop(0, layout.peers * layout.late, clear, 0)
     fill = pltpu.make_async_copy(zeros, blank, blank_sem)
     fill.start()
 
@@ -279,6 +292,11 @@
         def use(number, code, place):
             places[source * layout.block + number] = place
 
+            @pl.when(place >= layout.early)
+            def _():
+                late_index = source * layout.late + place - layout.early
+                numbers[late_index] = source * layout.block + number
+
         layout.visit(table, perm, source, me[0], page_len, use)
         return carry
 
@@ -286,15 +304,14 @@
     fill.wait()
 
     def inward(index):
-        spot = lax.rem(index, BUFFERS)
+        spot = index & (BUFFERS - 1)
         place = jnp.clip(places[index], 0, layout.early - 1)
         return pltpu.make_async_copy(
             arrived.at[lax.div(index, layout.block), place], buffers.at[spot], in_sems.at[spot]
         )
 
     def outward(index, held):
-        target = out.at[lax.div(index, layout.block), lax.rem(index, layout.block)]
-        return pltpu.make_async_copy(held, target, out_sems.at[lax.rem(index, BUFFERS)])
+        return pltpu.make_async_copy(held, out.at[index], out_sems.at[index & (BUFFERS - 1)])
 
     def is_early(index):
         return (places[index] >= 0) & (places[index] < layout.early)
@@ -308,7 +325,7 @@
         @pl.when(is_early(index))
         def _():
             inward(index).wait()
-            outward(index, buffers.at[lax.rem(index, BUFFERS)]).start()
+            outward(index, buffers.at[index & (BUFFERS - 1)]).start()
 
         @pl.when(places[index] < 0)
         def _():
@@ -322,37 +339,14 @@
     ring(layout.peers * layout.block, load, store, drain)
 
 
-def place_late_kernel(layout, table, perm, me, arrived, held, out, numbers, buffers, in_sems, out_sems):
-    page_len = buffers.shape[1]
-
-    def clear(index, carry):
-        numbers[index] = -1
-        return carry
-
-    lax.fori_loop(0, layout.peers * layout.late, clear, 0)
-
-    def block(source, carry):
-        def use(number, code, place):
-            @pl.when(place >= layout.early)
-            def _():
-                numbers[source * layout.late + place - layout.early] = number
-
-        layout.visit(table, perm, source, me[0], page_len, use)
-        return carry
-
-    lax.fori_loop(0, layout.peers, block, 0)
-
+def place_late_kernel(count, numbers, arrived, held, out, buffers, in_sems, out_sems):
     def inward(index):
-        spot = lax.rem(index, BUFFERS)
-        return pltpu.make_async_copy(
-            arrived.at[lax.div(index, layout.late), lax.rem(index, layout.late)],
-            buffers.at[spot],
-            in_sems.at[spot],
-        )
+        spot = index & (BUFFERS - 1)
+        return pltpu.make_async_copy(arrived.at[index], buffers.at[spot], in_sems.at[spot])
 
     def outward(index):
-        spot = lax.rem(index, BUFFERS)
-        target = out.at[lax.div(index, layout.late), jnp.maximum(numbers[index], 0)]
+        spot = index & (BUFFERS - 1)
+        target = out.at[jnp.maximum(numbers[index], 0)]
         return pltpu.make_async_copy(buffers.at[spot], target, out_sems.at[spot])
 
     def load(index):
@@ -371,19 +365,25 @@
         def _():
             outward(index).wait()
 
-    ring(layout.peers * layout.late, load, store, drain)
+    ring(count, load, store, drain)
 
 
 def place_early_pages(layout, table, perm, me, arrived, zeros):
     page = arrived.shape[2:]
     return pl.pallas_call(
         lambda *refs: place_kernel(layout, *refs),
-        out_shape=jax.ShapeDtypeStruct((layout.peers, layout.block) + page, arrived.dtype),
+        out_shape=(
+            jax.ShapeDtypeStruct((layout.peers * layout.block,) + page, arrived.dtype),
+            jax.ShapeDtypeStruct((layout.peers * layout.late,), jnp.int32),
+        ),
         grid_spec=pltpu.PrefetchScalarGridSpec(
             num_scalar_prefetch=3,
             grid=(1,),
             in_specs=[pl.BlockSpec(memory_space=pl.ANY)] * 2,
-            out_specs=pl.BlockSpec(memory_space=pl.ANY),
+            out_specs=(
+                pl.BlockSpec(memory_space=pl.ANY),
+                pl.BlockSpec(memory_space=pltpu.SMEM),
+            ),
             scratch_shapes=scratch(layout, arrived)
             + [pltpu.VMEM(page, arrived.dtype), pltpu.SemaphoreType.DMA],
         ),
@@ -391,20 +391,25 @@
     )(table, perm, me, arrived, zeros)
 
 
-def place_late_pages(layout, table, perm, me, arrived, held):
+def place_late_pages(numbers, arrived, held):
+    arrived = arrived.reshape((-1,) + held.shape[1:])
     return pl.pallas_call(
-        lambda *refs: place_late_kernel(layout, *refs),
+        lambda *refs: place_late_kernel(arrived.shape[0], *refs),
         out_shape=jax.ShapeDtypeStruct(held.shape, held.dtype),
         grid_spec=pltpu.PrefetchScalarGridSpec(
-            num_scalar_prefetch=3,
+            num_scalar_prefetch=1,
             grid=(1,),
             in_specs=[pl.BlockSpec(memory_space=pl.ANY)] * 2,
             out_specs=pl.BlockSpec(memory_space=pl.ANY),
-            scratch_shapes=scratch(layout, arrived),
+            scratch_shapes=[
+                pltpu.VMEM((BUFFERS,) + held.shape[1:], held.dtype),
+                pltpu.SemaphoreType.DMA((BUFFERS,)),
+                pltpu.SemaphoreType.DMA((BUFFERS,)),
+            ],
         ),
-        input_output_aliases={4: 0},
+        input_output_aliases={2: 0},
         name="place_late",
-    )(table, perm, me, arrived, held)
+    )(numbers, arrived, held)
 
 
 def attend_kernel(lengths, tables, q_ref, nk_ref, nv_ref, *rest):
@@ -587,9 +592,9 @@
         concat_axis=0,
         tiled=True,
     )
-    early_pages = place_early_pages(layout, table, perm, me, arrived, zeros)
-    decode_pages = place_late_pages(layout, table, perm, me, late_arrived, early_pages)
-    return (attn_out, decode_pages[None])
+    early_pages, numbers = place_early_pages(layout, table, perm, me, arrived, zeros)
+    decode_pages = place_late_pages(numbers, late_arrived, early_pages)
+    return (attn_out, decode_pages.reshape((1, peers, block) + pool.shape[1:]))
 
 
 def solution(mesh):

time: 454 us -> 448 us (0.987)
  Pallas kernels: 118 us -> 101 us
  waiting for transfers between devices: 243 us -> 256 us
    pallas_call x2, Pallas kernels: 27.2 us -> 17.5 us  [the longest x1 13.1 us: place_early_pages(): pl.pallas_call(lambda *refs: place_kernel(layout, *refs), out_shape=(jax....]
    all_to_all x1, waiting for transfers between devices: 168 us -> 176 us  [shards(): lax.all_to_all(outgoing, 'req', split_axis=0, concat_axis=0, tiled=True)]
    pallas_call x2, Pallas kernels: 29.9 us -> 22.3 us  [pack_pages(): pl.pallas_call(lambda *refs: pack_kernel(layout, late, *refs), out_shape=...]
    unnamed x22 -> x14, local copies, waits for them, and re-layouts: 10.1 us -> 9.33 us
  transfers between devices with their start and end apart: 4 -> 4, of which waited for: 2 -> 2; matrix products, arithmetic and copies ran while one was open for 13% -> 13% of each run, Pallas kernels for 20% -> 17%
where the time goes in v2:
time: 448 us; the launch traced here: 446 us
  waiting for transfers between devices  256 us (57%)
  Pallas kernels  101 us (23%)
  local copies, waits for them, and re-layouts  38.9 us (9%)
  matrix products  19 us (4%)
  between operations  14.3 us (3%)
  starting transfers between devices  11.5 us (3%)
  other arithmetic  5.69 us (1%)
    all_to_all x1, waiting for transfers between devices, shards(): lax.all_to_all(outgoing, 'req', split_axis=0, concat_axis=0, tiled=True)  176 us
    all_to_all x1, waiting for transfers between devices, shards(): lax.all_to_all(pack_pages(layout, table, perm, me, late_pool, recent, zer...  77.9 us
    pallas_call x1, Pallas kernels, attend(): pl.pallas_call(attend_kernel, out_shape=jax.ShapeDtypeStruct(queries.shap...  51.3 us
    pallas_call x2, Pallas kernels, pack_pages(): pl.pallas_call(lambda *refs: pack_kernel(layout, late, *refs), out_shape=...  22.3 us
    pallas_call x1, Pallas kernels, place_early_pages(): pl.pallas_call(lambda *refs: place_kernel(layout, *refs), out_shape=(jax....  13.1 us
    optimization_barrier x1, local copies, waits for them, and re-layouts, shards(): late_pool, wkv, outgoing = lax.optimization_barrier((pool, wkv, outgoing))  9.97 us
    pallas_call x1, Pallas kernels, exchange(): pl.pallas_call(lambda *refs: exchange_kernel(peers, *refs), out_shape=jax...  9.75 us
    unnamed x14, local copies, waits for them, and re-layouts  9.33 us
  transfers between devices with their start and end apart: 4, of which 2 were waited for; matrix products, arithmetic and copies ran while one was open for 13% of the time, Pallas kernels for 17%

profile of v2, /device:TPU:0, one launch (start us, length us, event | category | flops | bytes accessed | tf_op | source)
XLA Modules:
  0.0 446.0 jit_solution(607318196547626716)
XLA Ops:
  7.2 0.8 reshape.165
  7.9 0.8 reshape.164
  8.7 0.7 pad_add_fusion
  9.4 0.6 pad_bitcast_fusion.refs_0_
  10.0 9.8 %exchange.1 = s32[8,8,128]{2,1,0:T(8,128)} custom-call(s32[8,128]{1,0:T(8,128)} %pad_bitcast_fusion.refs_0_), custom_call_target="tpu_custom_call" | custom-call | tf_op jit(solution)/shard_map/exchange/pallas_call | solution.py:116
  19.8 15.3 %pack_early.1 = bf16[104,128,2,256]{3,2,1,0:T(2,128)(2,1)} custom-call(s32[8192]{0:T(1024)} %bitcast.60, s32[16]{0:T(128)} %refs_1_.5, s32[1]{0:T(128)} %bitcast.4.refs_2_, bf16[128,128,2,256]{3,2,1,0:T(2,128)(2,1)} %refs_3_.2), custom_call_target="tpu_custom_call" | custom-call | tf_op jit(solution)/shard_map/pack_early/pallas_call | solution.py:265
  35.1 6.9 %all-to-all-start = ((bf16[8,13,128,2,256]{4,3,2,1,0:T(2,128)(2,1)}), bf16[8,13,128,2,256]{4,3,2,1,0:T(2,128)(2,1)}, u32[]{:S(2)}, u32[]{:S(2)}) async-start(bf16[8,13,128,2,256]{4,3,2,1,0:T(2,128)(2,1)} %bitcast.50), calls=%async_computation.1 | async-start | bytes 27262976 | tf_op jit(solution)/shard_map/all_to_all | solution.py:552
  42.0 0.7 all-gather.2.cloned.1.call-update
  42.8 5.6 %copy.40 = bf16[640,8,2,256]{3,1,2,0:T(8,128)(2,1)} copy(bf16[640,8,2,256]{3,2,1,0:T(2,128)(2,1)} %bitcast.55) | data formatting | bytes 10485760
  48.5 8.0 %copy.22 = bf16[512,5120]{1,0:T(8,128)(2,1)} copy(bf16[512,5120]{0,1:T(8,128)(2,1)} %bitcast.51) | data formatting | bytes 10485760 | tf_op jit(solution)/shard_map/dot_general | solution.py:562
  56.6 0.6 gather_fusion
  57.3 0.3 multiply_cosine_fusion
  57.9 0.6 gather_fusion.1
  58.5 10.0 %copy.31 = bf16[128,128,2,256]{3,1,0,2:T(8,128)(2,1)S(1)} copy(bf16[128,128,2,256]{3,2,1,0:T(2,128)(2,1)} %refs_3_.2) | data formatting | bytes 33554432 | tf_op jit(solution)/shard_map/optimization_barrier | solution.py:555
  68.5 6.4 %slice_bitcast_fusion = (bf16[128,128,256]{2,1,0:T(8,128)(2,1)}, bf16[128,128,256]{2,1,0:T(8,128)(2,1)}) fusion(bf16[128,128,2,256]{3,1,0,2:T(8,128)(2,1)S(1)} %copy.31), kind=kLoop, calls=%fused_computation.2 | loop fusion | bytes 33554432 | tf_op jit(solution)/shard_map/squeeze | solution.py:580
  74.9 2.3 fusion
  77.3 5.1 %fusion.3 = f32[256,2,2,128]{0,3,2,1:T(8,128)S(1)} fusion(bf16[2,2,128,5120]{3,2,1,0:T(8,128)(2,1)} %bitcast.56, bf16[256,5120]{1,0:T(8,128)(2,1)} %all-gather.2.cloned.1.call-done, f32[5120]{0:T(1024)S(1)} %convert_element_type.65, f32[256]{0:T(256)S(1)} %add_rsqrt_fusion), kind=kOutput, calls=%fused_computation.9 | convolution fusion | flops 1347420160 | bytes 8410112 | tf_op jit(solution)/shard_map/dot_general | solution.py:562
  82.6 5.8 %convolution_bitcast_fusion = f32[32,8,8,128]{3,1,2,0:T(8,128)S(1)} fusion(bf16[5120,1024]{1,0:T(8,128)(2,1)} %param.12, bf16[256,5120]{1,0:T(8,128)(2,1)S(1)} %copy-done.1, f32[5120]{0:T(1024)S(1)} %convert_element_type.65, f32[256]{0:T(256)S(1)} %add_rsqrt_fusion), kind=kOutput, calls=%fused_computation.11 | convolution fusion | flops 2689597440 | bytes 14177280 | tf_op jit(solution)/shard_map/dot_general | solution.py:561
  88.6 0.5 subtract_convert_fusion
  89.1 0.3 pad_maximum_fusion
  90.1 3.4 copy-done
  93.5 51.3 %attend.1 = bf16[256,1024]{1,0:T(8,128)(2,1)S(1)} custom-call(s32[2]{0:T(128)S(1)} %gather_fusion, s32[128]{0:T(128)S(1)} %reshape.174.tables, bf16[256,1024]{1,0:T(8,128)(2,1)S(1)} %bitcast.49, bf16[256,256]{1,0:T(8,128)(2,1)S(1)} %copy.38.nk_ref, bf16[256,256]{1,0:T(8,128)(2,1)S(1)} %copy.39.nv_ref, bf16[128,128,256]{2,1,0:T(8,128)(2,1)S(1)} %copy-done, ...), custom_call_target="tpu_custom_call" | custom-call | tf_op jit(solution)/shard_map/attend/pallas_call | solution.py:502
  144.8 1.3 pad_maximum_fusion.1.refs_4_
  146.1 8.1 %fusion.7 = bf16[256,5120]{1,0:T(8,128)(2,1)} fusion(bf16[256,1024]{1,0:T(8,128)(2,1)S(1)} %attend.1, bf16[1024,5120]{1,0:T(8,128)(2,1)} %param.14), kind=kOutput, calls=%fused_computation.32 | convolution fusion | flops 2684354560 | bytes 13631488 | tf_op jit(solution)/shard_map/dot_general | solution.py:582
  154.2 0.7 broadcast_in_dim.5.refs_4_.refs_5_
  154.9 7.0 %pack_late.1 = bf16[32,128,2,256]{3,2,1,0:T(2,128)(2,1)} custom-call(s32[8192]{0:T(1024)} %bitcast.61, s32[16]{0:T(128)} %refs_1_.5, s32[1]{0:T(128)} %bitcast.4.refs_2_, bf16[128,128,2,256]{3,2,1,0:T(2,128)(2,1)} %refs_3_.2, bf16[2,128,2,256]{3,2,1,0:T(2,128)(2,1)} %pad_maximum_fusion.1.refs_4_, bf16[128,2,256]{2,1,0:T(2,128)(2,1)} %broadcast_in_dim.5.refs_4_.refs_5_), custom_call_target="tpu_custom_call" | custom-call | tf_op jit(solution)/shard_map/pack_late/pallas_call | solution.py:265
  161.9 176.5 %all-to-all-done.refs_3_ = bf16[8,13,128,2,256]{4,3,2,1,0:T(2,128)(2,1)} async-done(((bf16[8,13,128,2,256]{4,3,2,1,0:T(2,128)(2,1)}), bf16[8,13,128,2,256]{4,3,2,1,0:T(2,128)(2,1)}, u32[]{:S(2)}, u32[]{:S(2)}) %all-to-all-start) | async-done | bytes 13631520 | tf_op jit(solution)/shard_map/all_to_all | solution.py:552
  338.4 4.6 %all-to-all-start.1 = ((bf16[8,4,128,2,256]{4,3,2,1,0:T(2,128)(2,1)}), bf16[8,4,128,2,256]{4,3,2,1,0:T(2,128)(2,1)}, u32[]{:S(2)}, u32[]{:S(2)}) async-start(bf16[8,4,128,2,256]{4,3,2,1,0:T(2,128)(2,1)} %bitcast.53), calls=%async_computation.2 | async-start | bytes 8388608 | tf_op jit(solution)/shard_map/all_to_all | solution.py:588
  343.0 0.7 reduce-scatter.2.cloned.1.call-update
  343.7 13.1 %place_early.1 = (bf16[136,128,2,256]{3,2,1,0:T(2,128)(2,1)}, s32[32]{0:T(128)}) custom-call(s32[8192]{0:T(1024)} %bitcast.62, s32[16]{0:T(128)} %refs_1_.5, s32[1]{0:T(128)} %bitcast.4.refs_2_, bf16[8,13,128,2,256]{4,3,2,1,0:T(2,128)(2,1)} %all-to-all-done.refs_3_, bf16[128,2,256]{2,1,0:T(2,128)(2,1)} %broadcast_in_dim.5.refs_4_.refs_5_), custom_call_target="tpu_custom_call" | custom-call | tf_op jit(solution)/shard_map/place_early/pallas_call | solution.py:373
  356.8 77.9 %all-to-all-done.1 = bf16[8,4,128,2,256]{4,3,2,1,0:T(2,128)(2,1)} async-done(((bf16[8,4,128,2,256]{4,3,2,1,0:T(2,128)(2,1)}), bf16[8,4,128,2,256]{4,3,2,1,0:T(2,128)(2,1)}, u32[]{:S(2)}, u32[]{:S(2)}) %all-to-all-start.1) | async-done | bytes 4194336 | tf_op jit(solution)/shard_map/all_to_all | solution.py:588
  434.7 4.4 place_late.1
  (39 shorter events, 1.8 us)
Async XLA Ops:
  35.1 7.6 %copy-start.2 = (s32[8,8,128]{2,1,0:T(8,128)S(1)}, s32[8,8,128]{2,1,0:T(8,128)}, u32[]{:S(2)}) copy-start(s32[8,8,128]{2,1,0:T(8,128)} %exchange.1) | copy-start | bytes 98308
  35.1 303.3 %all-to-all-start = ((bf16[8,13,128,2,256]{4,3,2,1,0:T(2,128)(2,1)}), bf16[8,13,128,2,256]{4,3,2,1,0:T(2,128)(2,1)}, u32[]{:S(2)}, u32[]{:S(2)}) async-start(bf16[8,13,128,2,256]{4,3,2,1,0:T(2,128)(2,1)} %bitcast.50), calls=%async_computation.1 | async-start | bytes 27262976 | tf_op jit(solution)/shard_map/all_to_all | solution.py:552
  42.0 33.0 %all-gather.2.cloned.1.call-start = ((), (), s32[]{:S(2)}) async-start(), calls=%async_computation.3 | async-start | bytes 3276800 | tf_op jit(solution)/shard_map/all_gather | solution.py:554
  48.4 8.0 %copy-start.3 = (bf16[5120]{0:T(1024)(128)(2,1)S(1)}, bf16[5120]{0:T(1024)(128)(2,1)}, u32[]{:S(2)}) copy-start(bf16[5120]{0:T(1024)(128)(2,1)} %param.11) | copy-start | bytes 30724
  48.4 8.0 %copy-start.4 = (s32[16]{0:T(128)S(1)}, s32[16]{0:T(128)}, u32[]{:S(2)}) copy-start(s32[16]{0:T(128)} %refs_1_.5) | copy-start | bytes 196
  77.3 5.3 %copy-start.1 = (bf16[256,5120]{1,0:T(8,128)(2,1)S(1)}, bf16[256,5120]{1,0:T(8,128)(2,1)}, u32[]{:S(2)}) copy-start(bf16[256,5120]{1,0:T(8,128)(2,1)} %all-gather.2.cloned.1.call-done) | copy-start | bytes 7864324
  90.1 3.4 copy-start
  338.4 96.3 %all-to-all-start.1 = ((bf16[8,4,128,2,256]{4,3,2,1,0:T(2,128)(2,1)}), bf16[8,4,128,2,256]{4,3,2,1,0:T(2,128)(2,1)}, u32[]{:S(2)}, u32[]{:S(2)}) async-start(bf16[8,4,128,2,256]{4,3,2,1,0:T(2,128)(2,1)} %bitcast.53), calls=%async_computation.2 | async-start | bytes 8388608 | tf_op jit(solution)/shard_map/all_to_all | solution.py:588
  343.0 96.1 %reduce-scatter.2.cloned.1.call-start = ((), (), s32[]{:S(2)}) async-start(), calls=%async_computation.4 | async-start | bytes 3276800 | tf_op jit(solution)/shard_map/reduce_scatter | solution.py:584
Sparse Core Ops, SparseCore 0:
  44.4 26.9 all-gather.1
  346.9 35.9 reduce-scatter.1
